TPU v7x, 32 devices: a whole 2x2x4 slice. The times are simulated.
32 devices in a mesh: groups: 2 (over y), patch: 8 (over z, x), batch: 2 (over core).
Axes of the slice: x: 2, y: 2, z: 4, core: 2. Of those that a mesh axis runs over, the one named last changes fastest.
Arguments:
- subjects: bfloat16 [2048, 3, 20480], P(('groups', 'batch'), None, 'patch'), parts along dimension 0, may hold values from -6 to 6
- basis_modes: bfloat16 [3, 40960, 128], P(None, ('groups', 'patch')), parts along dimension 1, may hold values from -21 to 21
- laplace_blocks: bfloat16 [320, 4, 64, 64], P('patch'), may hold values from -0.29882812 to 0.29882812
- columns: int32 [320, 4], P('patch'), may hold values from 0 to 319, as said below
Outputs:
- scores: float32 [2048, 128], P(('groups', 'batch')), parts along dimension 0
- new_modes: bfloat16 [3, 40960, 128], P(None, ('groups', 'patch')), parts along dimension 1
- mode_norms: float32 [256], P('groups'), parts along dimension 0
There are 2 independent parts, one for each index of `groups`. A program takes and returns all parts, laid end to end along the dimension named above; an argument that names none is the same for every part. Nothing has to cross between parts.
Inputs may be any that keep to these rules, and one draw needn't show every extreme that they name: columns[i, 0] = i; with 40 blocks a patch, an entry of block row i lies in i's own patch, except that in the last 4 block rows of a patch an entry may also lie among the first 4 blocks of the next patch; entries of a row may repeat.
All inputs are finite; a program needn't handle non-finite values.
Results may differ from a plain program's by a relative error of at most 0.0034.
Values may be sent and summed in bfloat16 or wider, within the bound.
A program may use at most 192 MiB of HBM per device.

v0:
```python
import functools
import math

import jax
import jax.numpy as jnp
from jax import lax
from jax.experimental import pallas as pl
from jax.experimental.pallas import tpu as pltpu
from jax.sharding import PartitionSpec as P

GHOST = 4
MESH = pl.DeviceIdType.MESH
VMEM = pl.BlockSpec(memory_space=pltpu.VMEM)
ANY = pl.BlockSpec(memory_space=pl.ANY)
SMEM = pl.BlockSpec(memory_space=pltpu.SMEM)
LIMIT = 60 * 1024 * 1024


def greet(axes):
    barrier = pltpu.get_barrier_semaphore()
    peers = 0
    for axis in axes:
        n, me = lax.axis_size(axis), lax.axis_index(axis)
        for step in range(1, n):
            pl.semaphore_signal(
                barrier, inc=1, device_id={axis: lax.rem(me + step, n)}, device_id_type=MESH
            )
        peers += n - 1
    pl.semaphore_wait(barrier, peers)


def sum_kernel(
    n, scale, part_ref, modes, low_ref, turned_ref, after,
    land, full, send_a, recv_a, send_b, recv_b, send_c, recv_c,
):
    greet(("patch",))
    me = lax.axis_index("patch")
    rows = part_ref.shape[0] // n

    def start(source, target, to, send, recv):
        copy = pltpu.make_async_remote_copy(
            src_ref=source,
            dst_ref=target,
            send_sem=send,
            recv_sem=recv,
            device_id={"patch": to},
            device_id_type=MESH,
        )
        copy.start()
        return copy

    copies = []
    for step in range(1, n):
        to = lax.rem(me + step, n)
        source = part_ref.at[pl.ds(pl.multiple_of(to * rows, rows), rows)]
        copies.append(start(source, land.at[step], to, send_a.at[step], recv_a.at[step]))
    edge = pltpu.make_async_remote_copy(
        src_ref=modes.at[:, pl.ds(0, after.shape[1])],
        dst_ref=after,
        send_sem=send_c,
        recv_sem=recv_c,
        device_id={"patch": lax.rem(me + n - 1, n)},
        device_id_type=MESH,
    )

    @pl.when(me > 0)
    def _():
        edge.start()

    @pl.when(me == n - 1)
    def _():
        after[...] = jnp.zeros_like(after)

    own = pl.ds(pl.multiple_of(me * rows, rows), rows)
    total = part_ref[own, :]
    for step, copy in enumerate(copies, 1):
        copy.wait()
        total = total + land[step]
    full[own, :] = (total * scale).astype(jnp.bfloat16)
    copies = []
    for step in range(1, n):
        to = lax.rem(me + step, n)
        copies.append(start(full.at[own], full.at[own], to, send_b.at[step], recv_b.at[step]))
    for copy in copies:
        copy.wait()
    low_ref[...] = full[...]
    turned_ref[...] = full[...].astype(jnp.float32).T.astype(jnp.bfloat16)

    @pl.when(me > 0)
    def _():
        edge.wait_send()

    @pl.when(me < n - 1)
    def _():
        edge.wait_recv()


def reduce_scores(partial_value, basis_modes, reach, scale):
    n = lax.axis_size("patch")
    rows, width = partial_value.shape
    coords = basis_modes.shape[0]
    chunk = pltpu.VMEM((n, rows // n, width), jnp.float32)
    return pl.pallas_call(
        functools.partial(sum_kernel, n, scale),
        out_shape=(
            jax.ShapeDtypeStruct((rows, width), jnp.bfloat16),
            jax.ShapeDtypeStruct((width, rows), jnp.bfloat16),
            jax.ShapeDtypeStruct((coords, reach, width), jnp.bfloat16),
        ),
        in_specs=[VMEM, ANY],
        out_specs=(VMEM,) * 3,
        scratch_shapes=[chunk, pltpu.VMEM((rows, width), jnp.bfloat16)]
        + [pltpu.SemaphoreType.DMA((n,))] * 4
        + [pltpu.SemaphoreType.DMA] * 2,
        compiler_params=pltpu.CompilerParams(collective_id=0, has_side_effects=True),
        name="reduce_scores",
    )(partial_value, basis_modes)


def smooth_kernel(cols, blocks, modes, after, low, out, carry, scores, wide, acc):
    count, per_row, side, _ = blocks.shape
    coords, verts, width = modes.shape
    first = lax.axis_index("patch") * count
    scores[...] = low[...].astype(jnp.float32)
    ones = jnp.ones((wide.shape[0], width), jnp.bfloat16)
    for c in range(coords):
        lanes = slice(c * width, (c + 1) * width)
        wide[:verts, lanes] = modes[c]
        wide[verts:, lanes] = after[c]
    wide[:, coords * width :] = ones
    acc[...] = jnp.zeros_like(acc)

    def rows_of(block):
        return pl.ds(pl.multiple_of(block * side, side), side)

    def scatter(joined, block, targets):
        moved = lax.dot_general(
            joined,
            wide[rows_of(block), :],
            (((0,), (0,)), ((), ())),
            preferred_element_type=jnp.float32,
        )
        for slot, target in enumerate(targets):
            acc[rows_of(target), :] += moved[slot * side : (slot + 1) * side]

    group = math.gcd(count, 20)

    def step(outer, _):
        for inner in range(group):
            i = outer * group + inner
            joined = jnp.concatenate([blocks[i, slot] for slot in range(per_row)], axis=1)
            targets = [cols[slot, i] - first for slot in range(per_row)]
            picked = jnp.concatenate([wide[rows_of(t), :] for t in targets], axis=0)
            acc[rows_of(i), :] += jnp.dot(joined, picked, preferred_element_type=jnp.float32)
            scatter(joined, i, targets)
        return 0

    lax.fori_loop(0, count // group, step, 0)

    carry[...] = acc[verts:, :].astype(jnp.bfloat16)

    def finish(i, _):
        rows = rows_of(i)
        degree = acc[rows, coords * width :]
        for c in range(coords):
            mode = modes[c, rows, :].astype(jnp.float32)
            out[c, rows, :] = mode - 0.2 * (
                degree * mode - acc[rows, c * width : (c + 1) * width]
            )
        return 0

    lax.fori_loop(0, count, finish, 0)


def smoothed(basis_modes, laplace_blocks, columns, after, low):
    count, per_row, side, _ = laplace_blocks.shape
    coords, verts, width = basis_modes.shape
    reach = after.shape[1]
    lanes = (coords + 1) * width
    return pl.pallas_call(
        smooth_kernel,
        out_shape=(
            jax.ShapeDtypeStruct((coords, verts, width), jnp.float32),
            jax.ShapeDtypeStruct((reach, lanes), jnp.bfloat16),
            jax.ShapeDtypeStruct(low.shape, jnp.float32),
        ),
        in_specs=[SMEM] + [VMEM] * 4,
        out_specs=(VMEM,) * 3,
        scratch_shapes=[
            pltpu.VMEM((verts + reach, lanes), jnp.bfloat16),
            pltpu.VMEM((verts + reach, lanes), jnp.float32),
        ],
        compiler_params=pltpu.CompilerParams(vmem_limit_bytes=LIMIT),
        name="smooth",
    )(columns.T, laplace_blocks, basis_modes, after, low)


def update_kernel(
    scale, rate, coord_count, planes, base, modes, low, turned, carry, out, norms,
    held, updated, both, slots, extra, load, send_h, recv_h, send_n, recv_n, send_c, recv_c,
):
    n, me = lax.axis_size("patch"), lax.axis_index("patch")
    pair, half = lax.axis_size("batch"), lax.axis_index("batch")
    tiles, subjects, tile = held.shape
    coords, verts, width = modes.shape
    per = verts // tile
    loads = []
    for i in range(tiles):
        source = planes.at[i // per, :, pl.ds((i % per) * tile, tile)]
        loads.append(pltpu.make_async_copy(source, held.at[i], load.at[i]))
        loads[-1].start()
    loads.append(pltpu.make_async_copy(base, updated, load.at[tiles]))
    loads[-1].start()
    greet(("patch", "batch"))
    edge = pltpu.make_async_remote_copy(
        src_ref=carry,
        dst_ref=extra,
        send_sem=send_c,
        recv_sem=recv_c,
        device_id={"patch": lax.rem(me + 1, n)},
        device_id_type=MESH,
    )

    @pl.when(me < n - 1)
    def _():
        edge.start()

    @pl.when(me == 0)
    def _():
        extra[...] = jnp.zeros_like(extra)

    def residual_of(i):
        mode = modes[i // per, (i % per) * tile : (i % per + 1) * tile, :]
        recon = lax.dot_general(
            low[...], mode, (((1,), (1,)), ((), ())), preferred_element_type=jnp.float32
        )
        return (held[i].astype(jnp.float32) - recon * scale).astype(jnp.bfloat16)

    copies, ready = [], None
    for i in range(tiles + 1):
        if i < tiles:
            loads[i].wait()
            residual = residual_of(i)
        if i > 0:
            hebb = jnp.dot(turned[...], ready, preferred_element_type=jnp.float32)
            rows = pl.ds((i - 1) * tile, tile)
            both[half, rows, :] = hebb.T.astype(jnp.bfloat16)
            for step in range(1, pair):
                copy = pltpu.make_async_remote_copy(
                    src_ref=both.at[half, rows],
                    dst_ref=both.at[half, rows],
                    send_sem=send_h.at[step, i - 1],
                    recv_sem=recv_h.at[step, i - 1],
                    device_id={"batch": lax.rem(half + step, pair)},
                    device_id_type=MESH,
                )
                copy.start()
                copies.append(copy)
        ready = residual
    loads[tiles].wait()

    @pl.when(me < n - 1)
    def _():
        edge.wait_send()

    @pl.when(me > 0)
    def _():
        edge.wait_recv()

    reach = extra.shape[0]
    degree = extra[:, coords * width :].astype(jnp.float32)
    for c in range(coords):
        mode = modes[c, :reach, :].astype(jnp.float32)
        terms = degree * mode - extra[:, c * width : (c + 1) * width].astype(jnp.float32)
        updated[c * verts : c * verts + reach, :] += -0.2 * terms
    for copy in copies:
        copy.wait()

    piece = math.gcd(coords * verts, 256)

    def update(i, sums):
        here = pl.ds(pl.multiple_of(i * piece, piece), piece)
        hebb = both[0, here, :].astype(jnp.float32)
        for other in range(1, pair):
            hebb = hebb + both[other, here, :].astype(jnp.float32)
        value = updated[here, :] + rate * hebb
        updated[here, :] = value
        return sums + jnp.sum((value * value).reshape(piece // 8, 8, width), axis=0)

    count = coords * verts // piece
    slots[me] = lax.fori_loop(0, count, update, jnp.zeros((8, width), jnp.float32))
    copies = []
    for step in range(1, n):
        copy = pltpu.make_async_remote_copy(
            src_ref=slots.at[me],
            dst_ref=slots.at[me],
            send_sem=send_n.at[step],
            recv_sem=recv_n.at[step],
            device_id={"patch": lax.rem(me + step, n)},
            device_id_type=MESH,
        )
        copy.start()
        copies.append(copy)
    for copy in copies:
        copy.wait()
    squares = jnp.sum(jnp.sum(slots[...], axis=0), axis=0, keepdims=True)
    norm = jnp.sqrt(squares / coord_count + 1e-06)
    norms[...] = norm
    inverse = 1.0 / norm

    def divide(i, _):
        here = pl.ds(pl.multiple_of(i * piece, piece), piece)
        out[here, :] = (updated[here, :] * inverse).astype(jnp.bfloat16)
        return 0

    lax.fori_loop(0, count, divide, 0)


def updated_modes(planes, base, carry, basis_modes, low, turned, scale, rate, coord_count):
    n, pair = lax.axis_size("patch"), lax.axis_size("batch")
    coords, subjects, verts = planes.shape
    width = basis_modes.shape[2]
    rows = coords * verts
    tile = math.gcd(verts, 1280)
    tiles = rows // tile
    return pl.pallas_call(
        functools.partial(update_kernel, scale, rate, coord_count),
        out_shape=(
            jax.ShapeDtypeStruct((rows, width), jnp.bfloat16),
            jax.ShapeDtypeStruct((1, width), jnp.float32),
        ),
        in_specs=[ANY, ANY] + [VMEM] * 4,
        out_specs=(VMEM, VMEM),
        scratch_shapes=[
            pltpu.VMEM((tiles, subjects, tile), jnp.bfloat16),
            pltpu.VMEM((rows, width), jnp.float32),
            pltpu.VMEM((pair, rows, width), jnp.bfloat16),
            pltpu.VMEM((n, 8, width), jnp.float32),
            pltpu.VMEM(carry.shape, carry.dtype),
            pltpu.SemaphoreType.DMA((tiles + 1,)),
            pltpu.SemaphoreType.DMA((pair, tiles)),
            pltpu.SemaphoreType.DMA((pair, tiles)),
            pltpu.SemaphoreType.DMA((n,)),
            pltpu.SemaphoreType.DMA((n,)),
            pltpu.SemaphoreType.DMA,
            pltpu.SemaphoreType.DMA,
        ],
        compiler_params=pltpu.CompilerParams(
            collective_id=1, has_side_effects=True, vmem_limit_bytes=LIMIT
        ),
        name="update",
    )(planes, base.reshape(rows, width), basis_modes, low, turned, carry)


def body(subjects, basis_modes, laplace_blocks, columns):
    subject_count, coords, vert_count = subjects.shape
    mode_count = basis_modes.shape[2]
    batch = lax.axis_size("batch")
    coord_count = coords * vert_count * lax.axis_size("patch")
    scale_inv = 1.0 / math.sqrt(coord_count)
    planes = subjects.transpose(1, 0, 2)
    partial_value = lax.dot_general(
        subjects, basis_modes, (((1, 2), (0, 1)), ((), ())), preferred_element_type=jnp.float32
    )
    reach = GHOST * laplace_blocks.shape[2]
    low, turned, after = reduce_scores(partial_value, basis_modes, reach, scale_inv)
    base, carry, scores = smoothed(basis_modes, laplace_blocks, columns, after, low)
    rate = 4.0 / (subject_count * batch)
    new_modes, norms = updated_modes(
        planes, base, carry, basis_modes, low, turned, scale_inv, rate, coord_count
    )
    return (scores, new_modes.reshape(coords, vert_count, mode_count), norms.reshape(mode_count))


def solution(mesh):
    placed = (
        P(("groups", "batch"), None, "patch"),
        P(None, ("groups", "patch"), None),
        P("patch", None, None, None),
        P("patch", None),
    )
    return jax.shard_map(
        body,
        mesh=mesh,
        in_specs=placed,
        out_specs=(P(("groups", "batch"), None), P(None, ("groups", "patch"), None), P("groups")),
        check_vma=False,
    )
```

profile of v0, /device:TPU:0, one launch (start us, length us, event | category | flops | bytes accessed | tf_op | source)
XLA Modules:
  0.0 61.3 jit_solution(17699630324349497623)
XLA Ops:
  0.6 6.7 %convolution_bitcast_fusion.part_ref = f32[512,128]{1,0:T(8,128)} fusion(bf16[512,3,2560]{2,0,1:T(8,128)(2,1)} %param.4, bf16[3,2560,128]{2,1,0:T(8,128)(2,1)} %modes.5), kind=kOutput, calls=%fused_computation | convolution fusion | flops 1006632960 | bytes 10092544 | tf_op jit(solution)/shard_map/dot_general | solution.py:362
  7.3 21.0 %reduce_scores.1 = (bf16[512,128]{1,0:T(8,128)(2,1)}, bf16[128,512]{1,0:T(8,128)(2,1)}, bf16[3,256,128]{2,1,0:T(8,128)(2,1)}) custom-call(f32[512,128]{1,0:T(8,128)} %convolution_bitcast_fusion.part_ref, bf16[3,2560,128]{2,1,0:T(8,128)(2,1)} %modes.5), custom_call_target="tpu_custom_call" | custom-call | tf_op jit(solution)/shard_map/reduce_scores/pallas_call | solution.py:103
  28.3 10.2 %smooth.1 = (f32[3,2560,128]{2,1,0:T(8,128)}, bf16[256,512]{1,0:T(8,128)(2,1)}, f32[512,128]{1,0:T(8,128)}) custom-call(s32[4,40]{1,0:T(4,128)} %bitcast.12, bf16[40,4,64,64]{3,2,1,0:T(8,128)(2,1)} %blocks.1, bf16[3,2560,128]{2,1,0:T(8,128)(2,1)} %modes.5, bf16[3,256,128]{2,1,0:T(8,128)(2,1)} %get-tuple-element.11.after, bf16[512,128]{1,0:T(8,128)(2,1)} %get-tuple-element.12.low), custom_call_target="tpu_custom_call" | custom-call | tf_op jit(solution)/shard_map/smooth/pallas_call | solution.py:180
  38.5 19.3 %update.1 = (bf16[7680,128]{1,0:T(8,128)(2,1)}, f32[1,128]{1,0:T(1,128)}) custom-call(bf16[3,512,2560]{2,1,0:T(8,128)(2,1)} %bitcast.9, f32[7680,128]{1,0:T(8,128)} %bitcast.10, bf16[3,2560,128]{2,1,0:T(8,128)(2,1)} %modes.5, bf16[512,128]{1,0:T(8,128)(2,1)} %get-tuple-element.12.low, bf16[128,512]{1,0:T(8,128)(2,1)} %get-tuple-element.15.turned, ...), custom_call_target="tpu_custom_call" | custom-call | tf_op jit(solution)/shard_map/update/pallas_call | solution.py:326
  57.8 0.0 copy-start
  57.8 2.9 %copy.9 = bf16[3,2560,128]{2,1,0:T(8,128)(2,1)} copy(bf16[3,2560,128]{2,1,0:T(8,128)(2,1)} %bitcast.11) | data formatting | bytes 3932160
  60.7 0.0 copy-done
  60.8 0.5 copy.10
Async XLA Ops:
  57.8 3.0 %copy-start = (f32[1,128]{1,0:T(1,128)S(1)}, f32[1,128]{1,0:T(1,128)}, u32[]{:S(2)}) copy-start(f32[1,128]{1,0:T(1,128)} %get-tuple-element.18) | copy-start | bytes 1540
where the time goes:
time: 61.5 us; the launch traced here: 61.3 us
  Pallas kernels  50.5 us (82%)
  matrix products  6.68 us (11%)
  local copies, waits for them, and re-layouts  3.46 us (6%)
  between operations  0.66 us (1%)
    pallas_call x1, Pallas kernels, reduce_scores(): pl.pallas_call(functools.partial(sum_kernel, n, scale), out_shape=(jax.Sh...  21 us
    pallas_call x1, Pallas kernels, updated_modes(): pl.pallas_call(functools.partial(update_kernel, scale, rate, coord_count)...  19.3 us
    pallas_call x1, Pallas kernels, smoothed(): pl.pallas_call(smooth_kernel, out_shape=(jax.ShapeDtypeStruct((coords, ve...  10.2 us
    dot_general x1, matrix products, body(): lax.dot_general(subjects, basis_modes, (((1, 2), (0, 1)), ((), ())), pref...  6.68 us
    unnamed x4, local copies, waits for them, and re-layouts  3.46 us

commit v1 on v0

v1 whole, which is shorter than its diff:
```python
import functools
import math

import jax
import jax.numpy as jnp
from jax import lax
from jax.experimental import pallas as pl
from jax.experimental.pallas import tpu as pltpu
from jax.sharding import PartitionSpec as P

GHOST = 4
WIRE = jnp.bfloat16
MESH = pl.DeviceIdType.MESH
VMEM = pl.BlockSpec(memory_space=pltpu.VMEM)
ANY = pl.BlockSpec(memory_space=pl.ANY)
LIMIT = 62 * 1024 * 1024
FAR = (((1,), (1,)), ((), ()))
DOWN = (((0,), (0,)), ((), ()))


def ds(start, size):
    return pl.ds(pl.multiple_of(start, size), size)


def far_first(n):
    return sorted(range(1, n), key=lambda step: -min(step, n - step))


def dot(a, b):
    return jnp.dot(a, b, preferred_element_type=jnp.float32)


def step_kernel(
    scale, rate, coord_count,
    planes, modes, blocks, columns, table,
    updated, norms, low,
    held, wide, tail, lap, cols, links, part, outbox, land, run, acc, base, turned, flipped,
    outgo, income, carry, extra, slots,
    load_m, load_s, load_x, send_a, recv_a, send_b, recv_b, edge_sem, carry_sem,
    send_u, recv_u, send_g, recv_g, send_n, recv_n,
):
    n, me = lax.axis_size("patch"), lax.axis_index("patch")
    pair, half = lax.axis_size("batch"), lax.axis_index("batch")
    coords, subjects, verts = held.shape
    width = modes.shape[3]
    parts, rows, _ = part.shape
    own_rows = rows // n
    count, per_row, side, _ = lap.shape
    edge = tail.shape[0]
    lanes = coords * width
    share = verts // pair
    inner_blocks = count * pair
    first_row = half * count
    first = me * count * pair

    meta = [
        pltpu.make_async_copy(columns, cols, load_x.at[0]),
        pltpu.make_async_copy(table, links, load_x.at[1]),
        pltpu.make_async_copy(blocks.at[pl.ds(first_row, count)], lap, load_x.at[2]),
    ]
    mode_loads, loads = [], []
    for c in range(coords):
        mode_loads.append(
            pltpu.make_async_copy(
                modes.at[c],
                wide.at[pl.ds(0, inner_blocks), :, pl.ds(c * width, width)],
                load_m.at[c],
            )
        )
        mode_loads[-1].start()
        for j in range(parts):
            here = pl.ds(j * rows, rows)
            loads.append(
                pltpu.make_async_copy(planes.at[c, here], held.at[c, here], load_s.at[c, j])
            )
        loads[c * parts].start()
    for j in range(1, parts):
        for c in range(coords):
            loads[c * parts + j].start()
    for copy in meta:
        copy.start()

    barrier = pltpu.get_barrier_semaphore()
    for turn in range(pair):
        for step in range(n):
            if turn or step:
                pl.semaphore_signal(
                    barrier,
                    inc=1,
                    device_id={
                        "patch": lax.rem(me + step, n),
                        "batch": lax.rem(half + turn, pair),
                    },
                    device_id_type=MESH,
                )

    wide[:, :, lanes:] = jnp.ones((inner_blocks + edge, side, width), jnp.bfloat16)
    run[0] = jnp.zeros(run.shape[1:], jnp.float32)

    def modes_of(c):
        lane = slice(c * width, (c + 1) * width)
        return wide[:inner_blocks, :, lane].reshape(verts, width)

    scatters = []
    for j in range(parts):
        total = None
        for c in range(coords):
            if j == 0:
                mode_loads[c].wait()
            loads[c * parts + j].wait()
            term = dot(held[c, j * rows : (j + 1) * rows, :], modes_of(c))
            total = term if total is None else total + term
        part[j] = total
        outbox[j] = total.astype(WIRE)
        if j == 0:
            pl.semaphore_wait(barrier, n * pair - 1)
        block = []
        for step in far_first(n):
            to = lax.rem(me + step, n)
            block.append(
                pltpu.make_async_remote_copy(
                    src_ref=outbox.at[j, ds(to * own_rows, own_rows)],
                    dst_ref=land.at[j, step],
                    send_sem=send_a.at[j, step],
                    recv_sem=recv_a.at[j, step],
                    device_id={"patch": to},
                    device_id_type=MESH,
                )
            )
            block[-1].start()
        scatters.append(block)

    edge_copy = pltpu.make_async_remote_copy(
        src_ref=wide.at[pl.ds(0, edge), :, pl.ds(0, lanes)],
        dst_ref=tail,
        send_sem=edge_sem.at[0],
        recv_sem=edge_sem.at[1],
        device_id={"patch": lax.rem(me + n - 1, n), "batch": pair - 1},
        device_id_type=MESH,
    )
    gives_edge = jnp.logical_and(half == 0, me > 0)
    takes_edge = jnp.logical_and(half == pair - 1, me < n - 1)

    @pl.when(gives_edge)
    def _():
        edge_copy.start()

    @pl.when(jnp.logical_not(takes_edge))
    def _():
        tail[...] = jnp.zeros_like(tail)

    for copy in meta:
        copy.wait()
    dynamic = per_row - 1

    def block_rows(i):
        return ds(i * side, side)

    def smooth_row(i):
        mine = wide[first_row + i]
        joined = jnp.concatenate([lap[i, slot] for slot in range(per_row)], axis=1)
        targets = [
            jnp.maximum(cols[slot, first_row + i] - first, 0) for slot in range(1, per_row)
        ]
        picked = jnp.concatenate([mine] + [wide[t] for t in targets], axis=0)
        moved = lax.dot_general(joined, mine, DOWN, preferred_element_type=jnp.float32)
        acc[block_rows(i), :] = dot(joined, picked) + moved[:side]
        for slot in range(dynamic):
            before = links[slot + 1, first_row + i]
            entry = i * dynamic + slot + 1
            run[entry] = run[before] + moved[(slot + 1) * side : (slot + 2) * side]

    group = math.gcd(count - edge, 4)

    def smooth_group(outer, _):
        for inner in range(group):
            smooth_row(outer * group + inner)
        return 0

    lax.fori_loop(0, (count - edge) // group, smooth_group, 0)

    gathers = []
    for j in range(parts):
        own = ds(me * own_rows, own_rows)
        total = part[j, own, :]
        for copy, step in zip(scatters[j], far_first(n)):
            copy.wait()
            total = total + land[j, step].astype(jnp.float32)
        low[j, own, :] = (total * scale).astype(jnp.bfloat16)
        block = []
        for step in far_first(n):
            block.append(
                pltpu.make_async_remote_copy(
                    src_ref=low.at[j, own],
                    dst_ref=low.at[j, own],
                    send_sem=send_b.at[j, step],
                    recv_sem=recv_b.at[j, step],
                    device_id={"patch": lax.rem(me + step, n)},
                    device_id_type=MESH,
                )
            )
            block[-1].start()
        gathers.append(block)

    @pl.when(gives_edge)
    def _():
        edge_copy.wait_send()

    @pl.when(takes_edge)
    def _():
        edge_copy.wait_recv()

    wide[inner_blocks:, :, :lanes] = tail[...]
    for i in range(count - edge, count):
        smooth_row(i)

    carry_copy = pltpu.make_async_remote_copy(
        src_ref=carry,
        dst_ref=extra,
        send_sem=carry_sem.at[0],
        recv_sem=carry_sem.at[1],
        device_id={"patch": lax.rem(me + 1, n), "batch": 0},
        device_id_type=MESH,
    )
    gives_carry = takes_edge
    takes_carry = gives_edge
    for t in range(edge):
        sums = run[links[per_row + 1, t]]
        here = slice(t * side, (t + 1) * side)
        for c in range(coords):
            lane = slice(c * width, (c + 1) * width)
            mode = tail[t, :, lane].astype(jnp.float32)
            carry[c, here, :] = (sums[:, lanes:] * mode - sums[:, lane]).astype(jnp.bfloat16)

    @pl.when(gives_carry)
    def _():
        carry_copy.start()

    @pl.when(jnp.logical_not(takes_carry))
    def _():
        extra[...] = jnp.zeros_like(extra)

    def finish_own(i, _):
        sums = run[links[per_row, first_row + i]] + acc[block_rows(i), :]
        here = block_rows(first_row + i)
        for c in range(coords):
            lane = slice(c * width, (c + 1) * width)
            mode = wide[first_row + i, :, lane].astype(jnp.float32)
            base[c, here, :] = mode - 0.2 * (sums[:, lanes:] * mode - sums[:, lane])
        return 0

    lax.fori_loop(0, count, finish_own, 0)
    for turn in range(1, pair):
        far = lax.rem(half + turn, pair) * count

        def finish_other(i, _, far=far):
            sums = run[links[per_row, far + i]]
            here = block_rows(far + i)
            for c in range(coords):
                lane = slice(c * width, (c + 1) * width)
                mode = wide[far + i, :, lane].astype(jnp.float32)
                base[c, here, :] = -0.2 * (sums[:, lanes:] * mode - sums[:, lane])
            return 0

        lax.fori_loop(0, count, finish_other, 0)

    for c in range(coords):
        flipped[c] = modes_of(c).T

    for j in range(parts):
        for copy in gathers[j]:
            copy.wait()
        turned[:, j * rows : (j + 1) * rows] = low[j].astype(jnp.float32).T.astype(jnp.bfloat16)

    gram = lax.dot_general(turned[...], turned[...], FAR, preferred_element_type=jnp.float32)
    gram = gram * -scale
    gram_high = gram.astype(jnp.bfloat16)
    gram_low = (gram - gram_high.astype(jnp.float32)).astype(jnp.bfloat16)
    grams = jnp.concatenate([gram_high, gram_low], axis=1)
    tile = income.shape[2]
    per = share // tile

    def partial_update(c, start):
        here = ds(start, tile)
        across = flipped[c, :, here]
        hebb = dot(turned[...], held[c, :, here])
        hebb = hebb + dot(grams, jnp.concatenate([across, across], axis=0))
        return rate * hebb.T + base[c, here, :]

    exchanges = []
    for turn in range(1, pair):
        other = lax.rem(half + turn, pair)
        for k in range(coords * per):
            c, start = k // per, other * share + (k % per) * tile
            outgo[turn - 1, k] = partial_update(c, start).astype(jnp.bfloat16)
            exchanges.append(
                pltpu.make_async_remote_copy(
                    src_ref=outgo.at[turn - 1, k],
                    dst_ref=income.at[turn - 1, k],
                    send_sem=send_u.at[turn - 1, k],
                    recv_sem=recv_u.at[turn - 1, k],
                    device_id={"batch": other},
                    device_id_type=MESH,
                )
            )
            exchanges[-1].start()
    for k in range(coords * per):
        c, start = k // per, half * share + (k % per) * tile
        updated[ds(c * verts + start, tile), :] = partial_update(c, start)

    @pl.when(gives_carry)
    def _():
        carry_copy.wait_send()

    @pl.when(takes_carry)
    def _():
        carry_copy.wait_recv()

    @pl.when(half == 0)
    def _():
        for c in range(coords):
            here = pl.ds(c * verts, edge * side)
            updated[here, :] = updated[here, :] - 0.2 * extra[c].astype(jnp.float32)

    shares = []
    sums = jnp.zeros((8, width), jnp.float32)
    for k in range(coords * per):
        here = ds((k // per) * verts + half * share + (k % per) * tile, tile)
        value = updated[here, :]
        for turn in range(1, pair):
            exchanges[(turn - 1) * coords * per + k].wait()
            value = value + income[turn - 1, k].astype(jnp.float32)
        updated[here, :] = value
        sums = sums + jnp.sum((value * value).reshape(tile // 8, 8, width), axis=0)
        for turn in range(1, pair):
            shares.append(
                pltpu.make_async_remote_copy(
                    src_ref=updated.at[here],
                    dst_ref=updated.at[here],
                    send_sem=send_g.at[turn - 1, k],
                    recv_sem=recv_g.at[turn - 1, k],
                    device_id={"batch": lax.rem(half + turn, pair)},
                    device_id_type=MESH,
                )
            )
            shares[-1].start()
    mine = half * n + me
    slots[mine] = sums
    signals = []
    for turn in range(pair):
        for step in ([0] if turn else []) + far_first(n):
            at = turn * n + step
            signals.append(
                pltpu.make_async_remote_copy(
                    src_ref=slots.at[mine],
                    dst_ref=slots.at[mine],
                    send_sem=send_n.at[at],
                    recv_sem=recv_n.at[at],
                    device_id={
                        "patch": lax.rem(me + step, n),
                        "batch": lax.rem(half + turn, pair),
                    },
                    device_id_type=MESH,
                )
            )
            signals[-1].start()
    for copy in signals:
        copy.wait()
    squares = jnp.sum(jnp.sum(slots[...], axis=0), axis=0, keepdims=True)
    norms[...] = jnp.sqrt(squares / coord_count + 1e-06)
    for copy in shares:
        copy.wait()


def step(planes, modes, blocks, columns, table, scale, rate, coord_count):
    n, pair = lax.axis_size("patch"), lax.axis_size("batch")
    coords, subjects, verts = planes.shape
    width = modes.shape[2]
    all_rows, per_row, side, _ = blocks.shape
    modes = modes.reshape(coords, all_rows, side, width)
    count = all_rows // pair
    parts = max(1, min(4, subjects // (8 * n)))
    rows = subjects // parts
    reach = GHOST * side
    lanes = (coords + 1) * width
    share = verts // pair
    tile = math.gcd(share, 640)
    tiles = coords * share // tile
    dma = pltpu.SemaphoreType.DMA
    bf16, f32 = jnp.bfloat16, jnp.float32
    return pl.pallas_call(
        functools.partial(step_kernel, scale, rate, coord_count),
        out_shape=(
            jax.ShapeDtypeStruct((coords * verts, width), f32),
            jax.ShapeDtypeStruct((1, width), f32),
            jax.ShapeDtypeStruct((parts, rows, width), bf16),
        ),
        in_specs=[ANY] * 5,
        out_specs=(VMEM,) * 3,
        scratch_shapes=[
            pltpu.VMEM((coords, subjects, verts), bf16),
            pltpu.VMEM((all_rows + GHOST, side, lanes), bf16),
            pltpu.VMEM((GHOST, side, coords * width), bf16),
            pltpu.VMEM((count, per_row, side, side), bf16),
            pltpu.SMEM(columns.shape, jnp.int32),
            pltpu.SMEM(table.shape, jnp.int32),
            pltpu.VMEM((parts, rows, width), f32),
            pltpu.VMEM((parts, rows, width), WIRE),
            pltpu.VMEM((parts, n, rows // n, width), WIRE),
            pltpu.VMEM((1 + count * (per_row - 1), side, lanes), f32),
            pltpu.VMEM((count * side, lanes), f32),
            pltpu.VMEM((coords, verts, width), f32),
            pltpu.VMEM((width, subjects), bf16),
            pltpu.VMEM((coords, width, verts), bf16),
            pltpu.VMEM((pair - 1, tiles, tile, width), bf16),
            pltpu.VMEM((pair - 1, tiles, tile, width), bf16),
            pltpu.VMEM((coords, reach, width), bf16),
            pltpu.VMEM((coords, reach, width), bf16),
            pltpu.VMEM((n * pair, 8, width), f32),
            dma((coords,)),
            dma((coords, parts)),
            dma((3,)),
            dma((parts, n)),
            dma((parts, n)),
            dma((parts, n)),
            dma((parts, n)),
            dma((2,)),
            dma((2,)),
            dma((pair - 1, tiles)),
            dma((pair - 1, tiles)),
            dma((pair - 1, tiles)),
            dma((pair - 1, tiles)),
            dma((n * pair,)),
            dma((n * pair,)),
        ],
        compiler_params=pltpu.CompilerParams(
            collective_id=0, has_side_effects=True, vmem_limit_bytes=LIMIT
        ),
        name="step",
    )(planes, modes, blocks, columns, table)


def finish_kernel(updated, norm, low, out, norms, scores):
    inverse = 1.0 / norm[...]
    norms[...] = norm[...]
    scores[...] = low[...].astype(jnp.float32)
    rows = updated.shape[0]
    piece = math.gcd(rows, 256)

    def divide(i, _):
        here = ds(i * piece, piece)
        out[here, :] = (updated[here, :] * inverse).astype(jnp.bfloat16)
        return 0

    lax.fori_loop(0, rows // piece, divide, 0)


def finish(updated, norm, low):
    return pl.pallas_call(
        finish_kernel,
        out_shape=(
            jax.ShapeDtypeStruct(updated.shape, jnp.bfloat16),
            jax.ShapeDtypeStruct(norm.shape, jnp.float32),
            jax.ShapeDtypeStruct(low.shape, jnp.float32),
        ),
        in_specs=[VMEM] * 3,
        out_specs=(VMEM,) * 3,
        compiler_params=pltpu.CompilerParams(vmem_limit_bytes=16 * 1024 * 1024),
        name="finish",
    )(updated, norm, low)


def link_table(turned, first, pair, half):
    per_row, rows = turned.shape
    count = rows // pair
    slot = lax.broadcasted_iota(jnp.int32, (per_row + 2, rows), 0)
    row = lax.broadcasted_iota(jnp.int32, (per_row + 2, rows), 1)
    ends = (slot - per_row) * rows + row
    key = jnp.where(slot < per_row, jnp.pad(turned - first, ((0, 2), (0, 0))), ends)
    number = jnp.where(slot < per_row, (row - half * count) * (per_row - 1) + slot, 1 << 30)
    there = turned - first
    entry = number[:per_row]
    valid = (slot[:per_row] > 0) & (row[:per_row] // count == half)
    hits = (
        (there[:, :, None, None] == key[None, None])
        & valid[:, :, None, None]
        & (entry[:, :, None, None] < number[None, None])
    )
    return jnp.max(jnp.where(hits, entry[:, :, None, None], 0), axis=(0, 1))


def body(subjects, basis_modes, laplace_blocks, columns):
    subject_count, coords, vert_count = subjects.shape
    mode_count = basis_modes.shape[2]
    n, pair = lax.axis_size("patch"), lax.axis_size("batch")
    coord_count = coords * vert_count * n
    scale = 1.0 / math.sqrt(coord_count)
    rate = 4.0 / (subject_count * pair)
    planes = subjects.transpose(1, 0, 2)
    turned = columns.T
    first = lax.axis_index("patch") * laplace_blocks.shape[0]
    table = link_table(turned, first, pair, lax.axis_index("batch"))
    updated, norm, low = step(
        planes, basis_modes, laplace_blocks, turned, table, scale, rate, coord_count
    )
    low = low.reshape(subject_count, mode_count)
    new_modes, norms, scores = finish(updated, norm, low)
    return (scores, new_modes.reshape(coords, vert_count, mode_count), norms.reshape(mode_count))


def solution(mesh):
    placed = (
        P(("groups", "batch"), None, "patch"),
        P(None, ("groups", "patch"), None),
        P("patch", None, None, None),
        P("patch", None),
    )
    return jax.shard_map(
        body,
        mesh=mesh,
        in_specs=placed,
        out_specs=(P(("groups", "batch"), None), P(None, ("groups", "patch"), None), P("groups")),
        check_vma=False,
    )
```

time: 61.5 us -> 39.9 us (0.65)
  Pallas kernels: 50.5 us -> 33.6 us
  matrix products: 6.68 us -> 0 us
  other arithmetic: 0 us -> 1.72 us
    pallas_call x3 -> x2, Pallas kernels: 50.5 us -> 33.6 us  [the longest x1 31.9 us: step(): pl.pallas_call(functools.partial(step_kernel, scale, rate, coord_count),...]
    dot_general x1 -> x0, matrix products: 6.68 us -> none  [body(): lax.dot_general(subjects, basis_modes, (((1, 2), (0, 1)), ((), ())), pref...]
    reduce_max x0 -> x1, other arithmetic: none -> 0.85 us  [link_table(): return jnp.max(jnp.where(hits, entry[:, :, None, None], 0), axis=(0, 1))]
    sub x0 -> x1, other arithmetic: none -> 0.68 us  [link_table(): there = turned - first]
    unnamed x4 -> x6, local copies, waits for them, and re-layouts: 3.46 us -> 3.68 us
where the time goes in v1:
time: 39.9 us; the launch traced here: 39.7 us
  Pallas kernels  33.6 us (84%)
  local copies, waits for them, and re-layouts  3.69 us (9%)
  other arithmetic  1.72 us (4%)
  between operations  0.7 us (2%)
    pallas_call x1, Pallas kernels, step(): pl.pallas_call(functools.partial(step_kernel, scale, rate, coord_count),...  31.9 us
    unnamed x6, local copies, waits for them, and re-layouts  3.68 us
    pallas_call x1, Pallas kernels, finish(): pl.pallas_call(finish_kernel, out_shape=(jax.ShapeDtypeStruct(updated.sha...  1.7 us
    reduce_max x1, other arithmetic, link_table(): return jnp.max(jnp.where(hits, entry[:, :, None, None], 0), axis=(0, 1))  0.85 us

profile of v1, /device:TPU:0, one launch (start us, length us, event | category | flops | bytes accessed | tf_op | source)
XLA Modules:
  0.0 39.7 jit_solution(6896061158125514601)
XLA Ops:
  0.7 0.1 fusion
  0.8 0.7 %broadcast_subtract_fusion = s32[4,40]{1,0:T(4,128)S(1)} fusion(s32[]{:T(128)S(6)} %mul.20, s32[40,4]{0,1:T(4,128)} %param.7), kind=kLoop, calls=%fused_computation.9 | loop fusion | flops 160 | bytes 1284 | tf_op jit(solution)/shard_map/sub | solution.py:481
  1.5 0.1 add_select_fusion.1
  1.6 0.8 %select_reduce_fusion.table = s32[6,40]{1,0:T(8,128)} fusion(s32[6,40]{1,0:T(8,128)S(1)} %get-tuple-element.16, s32[4,40]{1,0:T(4,128)S(1)} %slice.18, s32[6,40]{1,0:T(8,128)S(1)} %get-tuple-element.15, s32[4,40]{1,0:T(4,128)S(1)} %broadcast_subtract_fusion, pred[4,40]{1,0:T(4,128)(4,1)S(1)} %fusion), kind=kLoop, calls=%fused_computation | loop fusion | flops 230160 | bytes 4320 | tf_op jit(solution)/shard_map/reduce_max | solution.py:489
  2.4 31.9 %step.1 = (f32[7680,128]{1,0:T(8,128)}, f32[1,128]{1,0:T(1,128)}, bf16[4,128,128]{2,1,0:T(8,128)(2,1)}) custom-call(bf16[3,512,2560]{2,1,0:T(8,128)(2,1)} %bitcast.8, bf16[3,40,64,128]{3,2,1,0:T(8,128)(2,1)} %bitcast.9, bf16[40,4,64,64]{3,2,1,0:T(8,128)(2,1)} %blocks.1, s32[4,40]{1,0:T(4,128)} %bitcast.10, s32[6,40]{1,0:T(8,128)} %select_reduce_fusion.table), custom_call_target="tpu_custom_call" | custom-call | tf_op jit(solution)/shard_map/step/pallas_call | solution.py:391
  34.3 0.0 copy-start
  34.3 2.1 %copy-done = f32[7680,128]{1,0:T(8,128)S(1)} copy-done((f32[7680,128]{1,0:T(8,128)S(1)}, f32[7680,128]{1,0:T(8,128)}, u32[]{:S(2)}) %copy-start) | copy-done | bytes 3932184
  36.4 0.0 copy-start.1
  36.4 0.9 %copy-done.1 = bf16[4,128,128]{2,1,0:T(8,128)(2,1)S(1)} copy-done((bf16[4,128,128]{2,1,0:T(8,128)(2,1)S(1)}, bf16[4,128,128]{2,1,0:T(8,128)(2,1)}, u32[]{:S(2)}) %copy-start.1) | copy-done | bytes 131096
  37.3 0.0 copy-start.2
  37.3 0.7 %copy-done.2 = f32[1,128]{1,0:T(1,128)S(1)} copy-done((f32[1,128]{1,0:T(1,128)S(1)}, f32[1,128]{1,0:T(1,128)}, u32[]{:S(2)}) %copy-start.2) | copy-done | bytes 536
  38.0 1.7 %finish.1 = (bf16[7680,128]{1,0:T(8,128)(2,1)}, f32[1,128]{1,0:T(1,128)}, f32[512,128]{1,0:T(8,128)}) custom-call(f32[7680,128]{1,0:T(8,128)S(1)} %copy-done, f32[1,128]{1,0:T(1,128)S(1)} %copy-done.2, bf16[512,128]{1,0:T(8,128)(2,1)S(1)} %bitcast.7), custom_call_target="tpu_custom_call" | custom-call | tf_op jit(solution)/shard_map/finish/pallas_call | solution.py:459
  (8 shorter events, 0.0 us)
Async XLA Ops:
  34.3 2.1 %copy-start = (f32[7680,128]{1,0:T(8,128)S(1)}, f32[7680,128]{1,0:T(8,128)}, u32[]{:S(2)}) copy-start(f32[7680,128]{1,0:T(8,128)} %get-tuple-element.9.updated) | copy-start | bytes 11796484
  36.4 0.9 %copy-start.1 = (bf16[4,128,128]{2,1,0:T(8,128)(2,1)S(1)}, bf16[4,128,128]{2,1,0:T(8,128)(2,1)}, u32[]{:S(2)}) copy-start(bf16[4,128,128]{2,1,0:T(8,128)(2,1)} %get-tuple-element.11) | copy-start | bytes 393220
  37.3 0.7 %copy-start.2 = (f32[1,128]{1,0:T(1,128)S(1)}, f32[1,128]{1,0:T(1,128)}, u32[]{:S(2)}) copy-start(f32[1,128]{1,0:T(1,128)} %get-tuple-element.10.norm) | copy-start | bytes 1540

commit v2 on v1

--- a/solution.py
+++ b/solution.py
@@ -13,7 +13,8 @@
 MESH = pl.DeviceIdType.MESH
 VMEM = pl.BlockSpec(memory_space=pltpu.VMEM)
 ANY = pl.BlockSpec(memory_space=pl.ANY)
-LIMIT = 62 * 1024 * 1024
+HBM = pl.BlockSpec(memory_space=pltpu.HBM)
+LIMIT = 44 * 1024 * 1024
 FAR = (((1,), (1,)), ((), ()))
 DOWN = (((0,), (0,)), ((), ()))
 
@@ -32,9 +33,9 @@
 
 def step_kernel(
     scale, rate, coord_count,
-    planes, modes, blocks, columns, table,
+    planes, modes, blocks, columns,
     updated, norms, low,
-    held, wide, tail, lap, cols, links, part, outbox, land, run, acc, base, turned, flipped,
+    held, wide, tail, lap, cols, listed, before, last, befores, lasts, part, outbox, land, run, acc, base, turned, flipped,
     outgo, income, carry, extra, slots,
     load_m, load_s, load_x, send_a, recv_a, send_b, recv_b, edge_sem, carry_sem,
     send_u, recv_u, send_g, recv_g, send_n, recv_n,
@@ -55,9 +56,11 @@
 
     meta = [
         pltpu.make_async_copy(columns, cols, load_x.at[0]),
-        pltpu.make_async_copy(table, links, load_x.at[1]),
+        pltpu.make_async_copy(columns, listed, load_x.at[1]),
         pltpu.make_async_copy(blocks.at[pl.ds(first_row, count)], lap, load_x.at[2]),
     ]
+    meta[0].start()
+    meta[1].start()
     mode_loads, loads = [], []
     for c in range(coords):
         mode_loads.append(
@@ -77,8 +80,7 @@
     for j in range(1, parts):
         for c in range(coords):
             loads[c * parts + j].start()
-    for copy in meta:
-        copy.start()
+    meta[2].start()
 
     barrier = pltpu.get_barrier_semaphore()
     for turn in range(pair):
@@ -96,6 +98,31 @@
 
     wide[:, :, lanes:] = jnp.ones((inner_blocks + edge, side, width), jnp.bfloat16)
     run[0] = jnp.zeros(run.shape[1:], jnp.float32)
+
+    meta[0].wait()
+    meta[1].wait()
+    dynamic = per_row - 1
+    slots_of = lax.broadcasted_iota(jnp.int32, listed.shape, 0)
+    rows_of = lax.broadcasted_iota(jnp.int32, listed.shape, 1) - first_row
+    order = rows_of * dynamic + slots_of
+    wanted = listed[...] - first
+    ends = lax.broadcasted_iota(jnp.int32, last.shape, 0) * inner_blocks
+    ends = ends + lax.broadcasted_iota(jnp.int32, last.shape, 1)
+    previous, final = jnp.zeros_like(wanted), jnp.zeros_like(ends)
+    for i in range(count):
+        for slot in range(1, per_row):
+            entry = i * dynamic + slot
+            target = cols[slot, first_row + i] - first
+            previous = jnp.where((wanted == target) & (order > entry), entry, previous)
+            final = jnp.where(ends == target, entry, final)
+    before[...] = previous
+    last[...] = final
+    links = [
+        pltpu.make_async_copy(before, befores, load_x.at[3]),
+        pltpu.make_async_copy(last, lasts, load_x.at[4]),
+    ]
+    for copy in links:
+        copy.start()
 
     def modes_of(c):
         lane = slice(c * width, (c + 1) * width)
@@ -149,9 +176,9 @@
     def _():
         tail[...] = jnp.zeros_like(tail)
 
-    for copy in meta:
+    meta[2].wait()
+    for copy in links:
         copy.wait()
-    dynamic = per_row - 1
 
     def block_rows(i):
         return ds(i * side, side)
@@ -166,9 +193,9 @@
         moved = lax.dot_general(joined, mine, DOWN, preferred_element_type=jnp.float32)
         acc[block_rows(i), :] = dot(joined, picked) + moved[:side]
         for slot in range(dynamic):
-            before = links[slot + 1, first_row + i]
+            earlier = befores[slot + 1, first_row + i]
             entry = i * dynamic + slot + 1
-            run[entry] = run[before] + moved[(slot + 1) * side : (slot + 2) * side]
+            run[entry] = run[earlier] + moved[(slot + 1) * side : (slot + 2) * side]
 
     group = math.gcd(count - edge, 4)
 
@@ -225,7 +252,7 @@
     gives_carry = takes_edge
     takes_carry = gives_edge
     for t in range(edge):
-        sums = run[links[per_row + 1, t]]
+        sums = run[lasts[1, t]]
         here = slice(t * side, (t + 1) * side)
         for c in range(coords):
             lane = slice(c * width, (c + 1) * width)
@@ -241,7 +268,7 @@
         extra[...] = jnp.zeros_like(extra)
 
     def finish_own(i, _):
-        sums = run[links[per_row, first_row + i]] + acc[block_rows(i), :]
+        sums = run[lasts[0, first_row + i]] + acc[block_rows(i), :]
         here = block_rows(first_row + i)
         for c in range(coords):
             lane = slice(c * width, (c + 1) * width)
@@ -254,7 +281,7 @@
         far = lax.rem(half + turn, pair) * count
 
         def finish_other(i, _, far=far):
-            sums = run[links[per_row, far + i]]
+            sums = run[lasts[0, far + i]]
             here = block_rows(far + i)
             for c in range(coords):
                 lane = slice(c * width, (c + 1) * width)
@@ -306,7 +333,7 @@
             exchanges[-1].start()
     for k in range(coords * per):
         c, start = k // per, half * share + (k % per) * tile
-        updated[ds(c * verts + start, tile), :] = partial_update(c, start)
+        base[c, ds(start, tile), :] = partial_update(c, start)
 
     @pl.when(gives_carry)
     def _():
@@ -319,18 +346,19 @@
     @pl.when(half == 0)
     def _():
         for c in range(coords):
-            here = pl.ds(c * verts, edge * side)
-            updated[here, :] = updated[here, :] - 0.2 * extra[c].astype(jnp.float32)
+            here = pl.ds(0, edge * side)
+            base[c, here, :] = base[c, here, :] - 0.2 * extra[c].astype(jnp.float32)
 
     shares = []
     sums = jnp.zeros((8, width), jnp.float32)
     for k in range(coords * per):
-        here = ds((k // per) * verts + half * share + (k % per) * tile, tile)
-        value = updated[here, :]
+        start = half * share + (k % per) * tile
+        here = ds((k // per) * verts + start, tile)
+        value = base[k // per, ds(start, tile), :]
         for turn in range(1, pair):
             exchanges[(turn - 1) * coords * per + k].wait()
             value = value + income[turn - 1, k].astype(jnp.float32)
-        updated[here, :] = value
+        updated[here, :] = value.astype(jnp.bfloat16)
         sums = sums + jnp.sum((value * value).reshape(tile // 8, 8, width), axis=0)
         for turn in range(1, pair):
             shares.append(
@@ -372,7 +400,7 @@
         copy.wait()
 
 
-def step(planes, modes, blocks, columns, table, scale, rate, coord_count):
+def step(planes, modes, blocks, columns, scale, rate, coord_count):
     n, pair = lax.axis_size("patch"), lax.axis_size("batch")
     coords, subjects, verts = planes.shape
     width = modes.shape[2]
@@ -391,11 +419,11 @@
     return pl.pallas_call(
         functools.partial(step_kernel, scale, rate, coord_count),
         out_shape=(
-            jax.ShapeDtypeStruct((coords * verts, width), f32),
+            jax.ShapeDtypeStruct((coords * verts, width), bf16),
             jax.ShapeDtypeStruct((1, width), f32),
             jax.ShapeDtypeStruct((parts, rows, width), bf16),
         ),
-        in_specs=[ANY] * 5,
+        in_specs=[HBM] * 4,
         out_specs=(VMEM,) * 3,
         scratch_shapes=[
             pltpu.VMEM((coords, subjects, verts), bf16),
@@ -403,7 +431,11 @@
             pltpu.VMEM((GHOST, side, coords * width), bf16),
             pltpu.VMEM((count, per_row, side, side), bf16),
             pltpu.SMEM(columns.shape, jnp.int32),
-            pltpu.SMEM(table.shape, jnp.int32),
+            pltpu.VMEM(columns.shape, jnp.int32),
+            pltpu.VMEM(columns.shape, jnp.int32),
+            pltpu.VMEM((2, all_rows), jnp.int32),
+            pltpu.SMEM(columns.shape, jnp.int32),
+            pltpu.SMEM((2, all_rows), jnp.int32),
             pltpu.VMEM((parts, rows, width), f32),
             pltpu.VMEM((parts, rows, width), WIRE),
             pltpu.VMEM((parts, n, rows // n, width), WIRE),
@@ -419,7 +451,7 @@
             pltpu.VMEM((n * pair, 8, width), f32),
             dma((coords,)),
             dma((coords, parts)),
-            dma((3,)),
+            dma((5,)),
             dma((parts, n)),
             dma((parts, n)),
             dma((parts, n)),
@@ -437,7 +469,7 @@
             collective_id=0, has_side_effects=True, vmem_limit_bytes=LIMIT
         ),
         name="step",
-    )(planes, modes, blocks, columns, table)
+    )(*(pltpu.with_memory_space_constraint(x, pltpu.HBM) for x in (planes, modes, blocks, columns)))
 
 
 def finish_kernel(updated, norm, low, out, norms, scores):
@@ -449,7 +481,7 @@
 
     def divide(i, _):
         here = ds(i * piece, piece)
-        out[here, :] = (updated[here, :] * inverse).astype(jnp.bfloat16)
+        out[here, :] = (updated[here, :].astype(jnp.float32) * inverse).astype(jnp.bfloat16)
         return 0
 
     lax.fori_loop(0, rows // piece, divide, 0)
@@ -470,25 +502,6 @@
     )(updated, norm, low)
 
 
-def link_table(turned, first, pair, half):
-    per_row, rows = turned.shape
-    count = rows // pair
-    slot = lax.broadcasted_iota(jnp.int32, (per_row + 2, rows), 0)
-    row = lax.broadcasted_iota(jnp.int32, (per_row + 2, rows), 1)
-    ends = (slot - per_row) * rows + row
-    key = jnp.where(slot < per_row, jnp.pad(turned - first, ((0, 2), (0, 0))), ends)
-    number = jnp.where(slot < per_row, (row - half * count) * (per_row - 1) + slot, 1 << 30)
-    there = turned - first
-    entry = number[:per_row]
-    valid = (slot[:per_row] > 0) & (row[:per_row] // count == half)
-    hits = (
-        (there[:, :, None, None] == key[None, None])
-        & valid[:, :, None, None]
-        & (entry[:, :, None, None] < number[None, None])
-    )
-    return jnp.max(jnp.where(hits, entry[:, :, None, None], 0), axis=(0, 1))
-
-
 def body(subjects, basis_modes, laplace_blocks, columns):
     subject_count, coords, vert_count = subjects.shape
     mode_count = basis_modes.shape[2]
@@ -497,11 +510,8 @@
     scale = 1.0 / math.sqrt(coord_count)
     rate = 4.0 / (subject_count * pair)
     planes = subjects.transpose(1, 0, 2)
-    turned = columns.T
-    first = lax.axis_index("patch") * laplace_blocks.shape[0]
-    table = link_table(turned, first, pair, lax.axis_index("batch"))
     updated, norm, low = step(
-        planes, basis_modes, laplace_blocks, turned, table, scale, rate, coord_count
+        planes, basis_modes, laplace_blocks, columns.T, scale, rate, coord_count
     )
     low = low.reshape(subject_count, mode_count)
     new_modes, norms, scores = finish(updated, norm, low)

time: 39.9 us -> 32.7 us (0.82)
  local copies, waits for them, and re-layouts: 3.69 us -> 0 us
  other arithmetic: 1.72 us -> 0 us
  Pallas kernels: 33.6 us -> 31.9 us
    unnamed x6 -> x0, local copies, waits for them, and re-layouts: 3.68 us -> none
    pallas_call x1, Pallas kernels: 31.9 us -> 30 us  [step(): pl.pallas_call(functools.partial(step_kernel, scale, rate, coord_count),...]
    reduce_max x1 -> x0, other arithmetic: 0.85 us -> none  [link_table(): return jnp.max(jnp.where(hits, entry[:, :, None, None], 0), axis=(0, 1))]
    sub x1 -> x0, other arithmetic: 0.68 us -> none  [link_table(): there = turned - first]
where the time goes in v2:
time: 32.7 us; the launch traced here: 32.5 us
  Pallas kernels  31.9 us (98%)
  between operations  0.64 us (2%)
    pallas_call x1, Pallas kernels, step(): pl.pallas_call(functools.partial(step_kernel, scale, rate, coord_count),...  30 us
    pallas_call x1, Pallas kernels, finish(): pl.pallas_call(finish_kernel, out_shape=(jax.ShapeDtypeStruct(updated.sha...  1.84 us

profile of v2, /device:TPU:0, one launch (start us, length us, event | category | flops | bytes accessed | tf_op | source)
XLA Modules:
  0.0 32.5 jit_solution(11390497880825088649)
XLA Ops:
  0.6 30.0 %step.1 = (bf16[7680,128]{1,0:T(8,128)(2,1)S(1)}, f32[1,128]{1,0:T(1,128)S(1)}, bf16[4,128,128]{2,1,0:T(8,128)(2,1)S(1)}) custom-call(bf16[3,512,2560]{2,1,0:T(8,128)(2,1)} %bitcast.7, bf16[3,40,64,128]{3,2,1,0:T(8,128)(2,1)} %bitcast.8, bf16[40,4,64,64]{3,2,1,0:T(8,128)(2,1)} %blocks.1, s32[4,40]{1,0:T(4,128)} %bitcast.9), custom_call_target="tpu_custom_call" | custom-call | tf_op jit(solution)/shard_map/step/pallas_call | solution.py:419
  30.7 1.8 %finish.1 = (bf16[7680,128]{1,0:T(8,128)(2,1)}, f32[1,128]{1,0:T(1,128)}, f32[512,128]{1,0:T(8,128)}) custom-call(bf16[7680,128]{1,0:T(8,128)(2,1)S(1)} %get-tuple-element.9.updated, f32[1,128]{1,0:T(1,128)S(1)} %get-tuple-element.10.norm, bf16[512,128]{1,0:T(8,128)(2,1)S(1)} %bitcast.6), custom_call_target="tpu_custom_call" | custom-call | tf_op jit(solution)/shard_map/finish/pallas_call | solution.py:491

commit v3 on v2

--- a/solution.py
+++ b/solution.py
@@ -294,25 +294,40 @@
     for c in range(coords):
         flipped[c] = modes_of(c).T
 
-    for j in range(parts):
-        for copy in gathers[j]:
-            copy.wait()
-        turned[:, j * rows : (j + 1) * rows] = low[j].astype(jnp.float32).T.astype(jnp.bfloat16)
-
-    gram = lax.dot_general(turned[...], turned[...], FAR, preferred_element_type=jnp.float32)
-    gram = gram * -scale
-    gram_high = gram.astype(jnp.bfloat16)
-    gram_low = (gram - gram_high.astype(jnp.float32)).astype(jnp.bfloat16)
-    grams = jnp.concatenate([gram_high, gram_low], axis=1)
     tile = income.shape[2]
     per = share // tile
 
-    def partial_update(c, start):
-        here = ds(start, tile)
-        across = flipped[c, :, here]
-        hebb = dot(turned[...], held[c, :, here])
-        hebb = hebb + dot(grams, jnp.concatenate([across, across], axis=0))
-        return rate * hebb.T + base[c, here, :]
+    def arrive(blocks_of):
+        for j in blocks_of:
+            for copy in gathers[j]:
+                copy.wait()
+            turned[:, j * rows : (j + 1) * rows] = (
+                low[j].astype(jnp.float32).T.astype(jnp.bfloat16)
+            )
+        span = slice(blocks_of[0] * rows, (blocks_of[-1] + 1) * rows)
+        front = turned[:, span]
+        gram = lax.dot_general(front, front, FAR, preferred_element_type=jnp.float32)
+        gram = gram * -scale
+        high = gram.astype(jnp.bfloat16)
+        rest = (gram - high.astype(jnp.float32)).astype(jnp.bfloat16)
+        grams = jnp.concatenate([high, rest], axis=1)
+
+        def partial_update(c, start):
+            here = ds(start, tile)
+            across = flipped[c, :, here]
+            hebb = dot(front, held[c, span, here])
+            hebb = hebb + dot(grams, jnp.concatenate([across, across], axis=0))
+            return rate * hebb.T + base[c, here, :]
+
+        return partial_update
+
+    early = parts // 2
+    if early:
+        partial_update = arrive(list(range(early)))
+        for k in range(coords * verts // tile):
+            c, start = k * tile // verts, k * tile % verts
+            base[c, start : start + tile, :] = partial_update(c, start)
+    partial_update = arrive(list(range(early, parts)))
 
     exchanges = []
     for turn in range(1, pair):
@@ -373,7 +388,7 @@
             )
             shares[-1].start()
     mine = half * n + me
-    slots[mine] = sums
+    slots[mine] = jnp.sum(sums, axis=0, keepdims=True)
     signals = []
     for turn in range(pair):
         for step in ([0] if turn else []) + far_first(n):
@@ -394,7 +409,7 @@
             signals[-1].start()
     for copy in signals:
         copy.wait()
-    squares = jnp.sum(jnp.sum(slots[...], axis=0), axis=0, keepdims=True)
+    squares = jnp.sum(slots[...], axis=0)
     norms[...] = jnp.sqrt(squares / coord_count + 1e-06)
     for copy in shares:
         copy.wait()
@@ -448,7 +463,7 @@
             pltpu.VMEM((pair - 1, tiles, tile, width), bf16),
             pltpu.VMEM((coords, reach, width), bf16),
             pltpu.VMEM((coords, reach, width), bf16),
-            pltpu.VMEM((n * pair, 8, width), f32),
+            pltpu.VMEM((n * pair, 1, width), f32),
             dma((coords,)),
             dma((coords, parts)),
             dma((5,)),
@@ -472,22 +487,31 @@
     )(*(pltpu.with_memory_space_constraint(x, pltpu.HBM) for x in (planes, modes, blocks, columns)))
 
 
-def finish_kernel(updated, norm, low, out, norms, scores):
+def finish_kernel(updated, norm, low, out, norms, scores, held, wide, sems):
     inverse = 1.0 / norm[...]
     norms[...] = norm[...]
-    scores[...] = low[...].astype(jnp.float32)
-    rows = updated.shape[0]
-    piece = math.gcd(rows, 256)
-
-    def divide(i, _):
-        here = ds(i * piece, piece)
-        out[here, :] = (updated[here, :].astype(jnp.float32) * inverse).astype(jnp.bfloat16)
-        return 0
-
-    lax.fori_loop(0, rows // piece, divide, 0)
+    pieces, rows, _ = held.shape
+    wide[...] = low[...].astype(jnp.float32)
+    copies = [pltpu.make_async_copy(wide, scores, sems.at[pieces])]
+    copies[0].start()
+    piece = math.gcd(rows, 128)
+    for k in range(pieces):
+
+        def divide(i, _, k=k):
+            value = updated[ds(k * rows + i * piece, piece), :].astype(jnp.float32)
+            held[k, ds(i * piece, piece), :] = (value * inverse).astype(jnp.bfloat16)
+            return 0
+
+        lax.fori_loop(0, rows // piece, divide, 0)
+        copies.append(pltpu.make_async_copy(held.at[k], out.at[pl.ds(k * rows, rows)], sems.at[k]))
+        copies[-1].start()
+    for copy in copies:
+        copy.wait()
 
 
 def finish(updated, norm, low):
+    rows, width = updated.shape
+    pieces = 6
     return pl.pallas_call(
         finish_kernel,
         out_shape=(
@@ -496,7 +520,12 @@
             jax.ShapeDtypeStruct(low.shape, jnp.float32),
         ),
         in_specs=[VMEM] * 3,
-        out_specs=(VMEM,) * 3,
+        out_specs=(ANY, VMEM, ANY),
+        scratch_shapes=[
+            pltpu.VMEM((pieces, rows // pieces, width), jnp.bfloat16),
+            pltpu.VMEM(low.shape, jnp.float32),
+            pltpu.SemaphoreType.DMA((pieces + 1,)),
+        ],
         compiler_params=pltpu.CompilerParams(vmem_limit_bytes=16 * 1024 * 1024),
         name="finish",
     )(updated, norm, low)

time: 32.7 us -> 32.4 us (level)
    pallas_call x1, Pallas kernels: 30 us -> 29.6 us  [step(): pl.pallas_call(functools.partial(step_kernel, scale, rate, coord_count),...]
where the time goes in v3:
time: 32.4 us; the launch traced here: 32.3 us
  Pallas kernels  31.6 us (98%)
  between operations  0.64 us (2%)
    pallas_call x1, Pallas kernels, step(): pl.pallas_call(functools.partial(step_kernel, scale, rate, coord_count),...  29.6 us
    pallas_call x1, Pallas kernels, finish(): pl.pallas_call(finish_kernel, out_shape=(jax.ShapeDtypeStruct(updated.sha...  1.98 us

profile of v3, /device:TPU:0, one launch (start us, length us, event | category | flops | bytes accessed | tf_op | source)
XLA Modules:
  0.0 32.3 jit_solution(16825750728310711227)
XLA Ops:
  0.6 29.6 %step.1 = (bf16[7680,128]{1,0:T(8,128)(2,1)S(1)}, f32[1,128]{1,0:T(1,128)S(1)}, bf16[4,128,128]{2,1,0:T(8,128)(2,1)S(1)}) custom-call(bf16[3,512,2560]{2,1,0:T(8,128)(2,1)} %bitcast.7, bf16[3,40,64,128]{3,2,1,0:T(8,128)(2,1)} %bitcast.8, bf16[40,4,64,64]{3,2,1,0:T(8,128)(2,1)} %blocks.1, s32[4,40]{1,0:T(4,128)} %bitcast.9), custom_call_target="tpu_custom_call" | custom-call | tf_op jit(solution)/shard_map/step/pallas_call | solution.py:434
  30.3 2.0 %finish.1 = (bf16[7680,128]{1,0:T(8,128)(2,1)}, f32[1,128]{1,0:T(1,128)}, f32[512,128]{1,0:T(8,128)}) custom-call(bf16[7680,128]{1,0:T(8,128)(2,1)S(1)} %get-tuple-element.9.updated, f32[1,128]{1,0:T(1,128)S(1)} %get-tuple-element.10.norm, bf16[512,128]{1,0:T(8,128)(2,1)S(1)} %bitcast.6), custom_call_target="tpu_custom_call" | custom-call | tf_op jit(solution)/shard_map/finish/pallas_call | solution.py:515

commit v4 on v3

--- a/solution.py
+++ b/solution.py
@@ -23,6 +23,10 @@
     return pl.ds(pl.multiple_of(start, size), size)
 
 
+def eights(start, size):
+    return pl.ds(pl.multiple_of(start, 8), size)
+
+
 def far_first(n):
     return sorted(range(1, n), key=lambda step: -min(step, n - step))
 
@@ -32,7 +36,7 @@
 
 
 def step_kernel(
-    scale, rate, coord_count,
+    sizes, scale, rate, coord_count,
     planes, modes, blocks, columns,
     updated, norms, low,
     held, wide, tail, lap, cols, listed, before, last, befores, lasts, part, outbox, land, run, acc, base, turned, flipped,
@@ -44,8 +48,8 @@
     pair, half = lax.axis_size("batch"), lax.axis_index("batch")
     coords, subjects, verts = held.shape
     width = modes.shape[3]
-    parts, rows, _ = part.shape
-    own_rows = rows // n
+    parts = len(sizes)
+    starts = [sum(sizes[:j]) for j in range(parts)]
     count, per_row, side, _ = lap.shape
     edge = tail.shape[0]
     lanes = coords * width
@@ -72,7 +76,7 @@
         )
         mode_loads[-1].start()
         for j in range(parts):
-            here = pl.ds(j * rows, rows)
+            here = pl.ds(starts[j], sizes[j])
             loads.append(
                 pltpu.make_async_copy(planes.at[c, here], held.at[c, here], load_s.at[c, j])
             )
@@ -131,14 +135,16 @@
     scatters = []
     for j in range(parts):
         total = None
+        block_of = slice(starts[j], starts[j] + sizes[j])
+        own_rows = sizes[j] // n
         for c in range(coords):
             if j == 0:
                 mode_loads[c].wait()
             loads[c * parts + j].wait()
-            term = dot(held[c, j * rows : (j + 1) * rows, :], modes_of(c))
+            term = dot(held[c, block_of, :], modes_of(c))
             total = term if total is None else total + term
-        part[j] = total
-        outbox[j] = total.astype(WIRE)
+        part[block_of, :] = total
+        outbox[block_of, :] = total.astype(WIRE)
         if j == 0:
             pl.semaphore_wait(barrier, n * pair - 1)
         block = []
@@ -146,8 +152,8 @@
             to = lax.rem(me + step, n)
             block.append(
                 pltpu.make_async_remote_copy(
-                    src_ref=outbox.at[j, ds(to * own_rows, own_rows)],
-                    dst_ref=land.at[j, step],
+                    src_ref=outbox.at[eights(starts[j] + to * own_rows, own_rows)],
+                    dst_ref=land.at[step, pl.ds(starts[j] // n, own_rows)],
                     send_sem=send_a.at[j, step],
                     recv_sem=recv_a.at[j, step],
                     device_id={"patch": to},
@@ -208,18 +214,20 @@
 
     gathers = []
     for j in range(parts):
-        own = ds(me * own_rows, own_rows)
-        total = part[j, own, :]
+        own_rows = sizes[j] // n
+        own = eights(starts[j] + me * own_rows, own_rows)
+        total = part[own, :]
         for copy, step in zip(scatters[j], far_first(n)):
             copy.wait()
-            total = total + land[j, step].astype(jnp.float32)
-        low[j, own, :] = (total * scale).astype(jnp.bfloat16)
+            landed = slice(starts[j] // n, starts[j] // n + own_rows)
+            total = total + land[step, landed, :].astype(jnp.float32)
+        low[own, :] = (total * scale).astype(jnp.bfloat16)
         block = []
         for step in far_first(n):
             block.append(
                 pltpu.make_async_remote_copy(
-                    src_ref=low.at[j, own],
-                    dst_ref=low.at[j, own],
+                    src_ref=low.at[own],
+                    dst_ref=low.at[own],
                     send_sem=send_b.at[j, step],
                     recv_sem=recv_b.at[j, step],
                     device_id={"patch": lax.rem(me + step, n)},
@@ -301,10 +309,8 @@
         for j in blocks_of:
             for copy in gathers[j]:
                 copy.wait()
-            turned[:, j * rows : (j + 1) * rows] = (
-                low[j].astype(jnp.float32).T.astype(jnp.bfloat16)
-            )
-        span = slice(blocks_of[0] * rows, (blocks_of[-1] + 1) * rows)
+        span = slice(starts[blocks_of[0]], starts[blocks_of[-1]] + sizes[blocks_of[-1]])
+        turned[:, span] = low[span, :].astype(jnp.float32).T.astype(jnp.bfloat16)
         front = turned[:, span]
         gram = lax.dot_general(front, front, FAR, preferred_element_type=jnp.float32)
         gram = gram * -scale
@@ -423,7 +429,9 @@
     modes = modes.reshape(coords, all_rows, side, width)
     count = all_rows // pair
     parts = max(1, min(4, subjects // (8 * n)))
-    rows = subjects // parts
+    sizes = [subjects // parts] * parts
+    if parts == 4 and subjects % (64 * n) == 0:
+        sizes = [subjects // 8 * units for units in (2, 2, 3, 1)]
     reach = GHOST * side
     lanes = (coords + 1) * width
     share = verts // pair
@@ -432,11 +440,11 @@
     dma = pltpu.SemaphoreType.DMA
     bf16, f32 = jnp.bfloat16, jnp.float32
     return pl.pallas_call(
-        functools.partial(step_kernel, scale, rate, coord_count),
+        functools.partial(step_kernel, sizes, scale, rate, coord_count),
         out_shape=(
             jax.ShapeDtypeStruct((coords * verts, width), bf16),
             jax.ShapeDtypeStruct((1, width), f32),
-            jax.ShapeDtypeStruct((parts, rows, width), bf16),
+            jax.ShapeDtypeStruct((subjects, width), bf16),
         ),
         in_specs=[HBM] * 4,
         out_specs=(VMEM,) * 3,
@@ -451,9 +459,9 @@
             pltpu.VMEM((2, all_rows), jnp.int32),
             pltpu.SMEM(columns.shape, jnp.int32),
             pltpu.SMEM((2, all_rows), jnp.int32),
-            pltpu.VMEM((parts, rows, width), f32),
-            pltpu.VMEM((parts, rows, width), WIRE),
-            pltpu.VMEM((parts, n, rows // n, width), WIRE),
+            pltpu.VMEM((subjects, width), f32),
+            pltpu.VMEM((subjects, width), WIRE),
+            pltpu.VMEM((n, subjects // n, width), WIRE),
             pltpu.VMEM((1 + count * (per_row - 1), side, lanes), f32),
             pltpu.VMEM((count * side, lanes), f32),
             pltpu.VMEM((coords, verts, width), f32),
@@ -494,15 +502,9 @@
     wide[...] = low[...].astype(jnp.float32)
     copies = [pltpu.make_async_copy(wide, scores, sems.at[pieces])]
     copies[0].start()
-    piece = math.gcd(rows, 128)
     for k in range(pieces):
-
-        def divide(i, _, k=k):
-            value = updated[ds(k * rows + i * piece, piece), :].astype(jnp.float32)
-            held[k, ds(i * piece, piece), :] = (value * inverse).astype(jnp.bfloat16)
-            return 0
-
-        lax.fori_loop(0, rows // piece, divide, 0)
+        value = updated[k * rows : (k + 1) * rows, :].astype(jnp.float32)
+        held[k] = (value * inverse).astype(jnp.bfloat16)
         copies.append(pltpu.make_async_copy(held.at[k], out.at[pl.ds(k * rows, rows)], sems.at[k]))
         copies[-1].start()
     for copy in copies:
@@ -542,7 +544,6 @@
     updated, norm, low = step(
         planes, basis_modes, laplace_blocks, columns.T, scale, rate, coord_count
     )
-    low = low.reshape(subject_count, mode_count)
     new_modes, norms, scores = finish(updated, norm, low)
     return (scores, new_modes.reshape(coords, vert_count, mode_count), norms.reshape(mode_count))
 

time: 32.4 us -> 32.3 us (level)
  no operation moved by 1% of the time
where the time goes in v4:
time: 32.3 us; the launch traced here: 32.2 us
  Pallas kernels  31.5 us (98%)
  between operations  0.64 us (2%)
    pallas_call x1, Pallas kernels, step(): pl.pallas_call(functools.partial(step_kernel, sizes, scale, rate, coord_c...  29.6 us
    pallas_call x1, Pallas kernels, finish(): pl.pallas_call(finish_kernel, out_shape=(jax.ShapeDtypeStruct(updated.sha...  1.94 us

profile of v4, /device:TPU:0, one launch (start us, length us, event | category | flops | bytes accessed | tf_op | source)
XLA Modules:
  0.0 32.2 jit_solution(16063385561369251225)
XLA Ops:
  0.6 29.6 %step.1 = (bf16[7680,128]{1,0:T(8,128)(2,1)S(1)}, f32[1,128]{1,0:T(1,128)S(1)}, bf16[512,128]{1,0:T(8,128)(2,1)S(1)}) custom-call(bf16[3,512,2560]{2,1,0:T(8,128)(2,1)} %bitcast.5, bf16[3,40,64,128]{3,2,1,0:T(8,128)(2,1)} %bitcast.6, bf16[40,4,64,64]{3,2,1,0:T(8,128)(2,1)} %blocks.1, s32[4,40]{1,0:T(4,128)} %bitcast.7), custom_call_target="tpu_custom_call" | custom-call | tf_op jit(solution)/shard_map/step/pallas_call | solution.py:442
  30.2 1.9 %finish.1 = (bf16[7680,128]{1,0:T(8,128)(2,1)}, f32[1,128]{1,0:T(1,128)}, f32[512,128]{1,0:T(8,128)}) custom-call(bf16[7680,128]{1,0:T(8,128)(2,1)S(1)} %get-tuple-element.9.updated, f32[1,128]{1,0:T(1,128)S(1)} %get-tuple-element.10.norm, bf16[512,128]{1,0:T(8,128)(2,1)S(1)} %get-tuple-element.11.low), custom_call_target="tpu_custom_call" | custom-call | tf_op jit(solution)/shard_map/finish/pallas_call | solution.py:517

commit v5 on v4

--- a/solution.py
+++ b/solution.py
@@ -435,7 +435,7 @@
     reach = GHOST * side
     lanes = (coords + 1) * width
     share = verts // pair
-    tile = math.gcd(share, 640)
+    tile = math.gcd(share, 256)
     tiles = coords * share // tile
     dma = pltpu.SemaphoreType.DMA
     bf16, f32 = jnp.bfloat16, jnp.float32

time: 32.3 us -> 34.4 us (1.065)
  Pallas kernels: 31.5 us -> 33.6 us
    pallas_call x1, Pallas kernels: 29.6 us -> 31.7 us  [step(): pl.pallas_call(functools.partial(step_kernel, sizes, scale, rate, coord_c...]
where the time goes in v5:
time: 34.4 us; the launch traced here: 34.3 us
  Pallas kernels  33.6 us (98%)
  between operations  0.64 us (2%)
    pallas_call x1, Pallas kernels, step(): pl.pallas_call(functools.partial(step_kernel, sizes, scale, rate, coord_c...  31.7 us
    pallas_call x1, Pallas kernels, finish(): pl.pallas_call(finish_kernel, out_shape=(jax.ShapeDtypeStruct(updated.sha...  1.94 us

profile of v5, /device:TPU:0, one launch (start us, length us, event | category | flops | bytes accessed | tf_op | source)
XLA Modules:
  0.0 34.3 jit_solution(8843000019734870779)
XLA Ops:
  0.6 31.7 %step.1 = (bf16[7680,128]{1,0:T(8,128)(2,1)S(1)}, f32[1,128]{1,0:T(1,128)S(1)}, bf16[512,128]{1,0:T(8,128)(2,1)S(1)}) custom-call(bf16[3,512,2560]{2,1,0:T(8,128)(2,1)} %bitcast.5, bf16[3,40,64,128]{3,2,1,0:T(8,128)(2,1)} %bitcast.6, bf16[40,4,64,64]{3,2,1,0:T(8,128)(2,1)} %blocks.1, s32[4,40]{1,0:T(4,128)} %bitcast.7), custom_call_target="tpu_custom_call" | custom-call | tf_op jit(solution)/shard_map/step/pallas_call | solution.py:442
  32.3 1.9 %finish.1 = (bf16[7680,128]{1,0:T(8,128)(2,1)}, f32[1,128]{1,0:T(1,128)}, f32[512,128]{1,0:T(8,128)}) custom-call(bf16[7680,128]{1,0:T(8,128)(2,1)S(1)} %get-tuple-element.9.updated, f32[1,128]{1,0:T(1,128)S(1)} %get-tuple-element.10.norm, bf16[512,128]{1,0:T(8,128)(2,1)S(1)} %get-tuple-element.11.low), custom_call_target="tpu_custom_call" | custom-call | tf_op jit(solution)/shard_map/finish/pallas_call | solution.py:517

commit v6 on v5

--- a/solution.py
+++ b/solution.py
@@ -435,7 +435,7 @@
     reach = GHOST * side
     lanes = (coords + 1) * width
     share = verts // pair
-    tile = math.gcd(share, 256)
+    tile = math.gcd(share, 1280)
     tiles = coords * share // tile
     dma = pltpu.SemaphoreType.DMA
     bf16, f32 = jnp.bfloat16, jnp.float32

time: 34.4 us -> 31.5 us (0.916)
  Pallas kernels: 33.6 us -> 30.7 us
    pallas_call x1, Pallas kernels: 31.7 us -> 28.8 us  [step(): pl.pallas_call(functools.partial(step_kernel, sizes, scale, rate, coord_c...]
where the time goes in v6:
time: 31.5 us; the launch traced here: 31.4 us
  Pallas kernels  30.7 us (97%)
  between operations  0.64 us (2%)
    pallas_call x1, Pallas kernels, step(): pl.pallas_call(functools.partial(step_kernel, sizes, scale, rate, coord_c...  28.8 us
    pallas_call x1, Pallas kernels, finish(): pl.pallas_call(finish_kernel, out_shape=(jax.ShapeDtypeStruct(updated.sha...  1.94 us

profile of v6, /device:TPU:0, one launch (start us, length us, event | category | flops | bytes accessed | tf_op | source)
XLA Modules:
  0.0 31.4 jit_solution(16821678103436147329)
XLA Ops:
  0.6 28.8 %step.1 = (bf16[7680,128]{1,0:T(8,128)(2,1)S(1)}, f32[1,128]{1,0:T(1,128)S(1)}, bf16[512,128]{1,0:T(8,128)(2,1)S(1)}) custom-call(bf16[3,512,2560]{2,1,0:T(8,128)(2,1)} %bitcast.5, bf16[3,40,64,128]{3,2,1,0:T(8,128)(2,1)} %bitcast.6, bf16[40,4,64,64]{3,2,1,0:T(8,128)(2,1)} %blocks.1, s32[4,40]{1,0:T(4,128)} %bitcast.7), custom_call_target="tpu_custom_call" | custom-call | tf_op jit(solution)/shard_map/step/pallas_call | solution.py:442
  29.4 1.9 %finish.1 = (bf16[7680,128]{1,0:T(8,128)(2,1)}, f32[1,128]{1,0:T(1,128)}, f32[512,128]{1,0:T(8,128)}) custom-call(bf16[7680,128]{1,0:T(8,128)(2,1)S(1)} %get-tuple-element.9.updated, f32[1,128]{1,0:T(1,128)S(1)} %get-tuple-element.10.norm, bf16[512,128]{1,0:T(8,128)(2,1)S(1)} %get-tuple-element.11.low), custom_call_target="tpu_custom_call" | custom-call | tf_op jit(solution)/shard_map/finish/pallas_call | solution.py:517
